TPU v7x, 128 devices: a whole 4x4x4 slice. The times are simulated.
128 devices in a mesh: row: 16 (over y, z_hi, core), col: 8 (over x, z_lo).
Axes of the slice: x: 4, y: 4, z: 4 (z_hi: 2, z_lo: 2; z = z_hi * 2 + z_lo), core: 2. Of those that a mesh axis runs over, the one named last changes fastest.
Arguments:
- orbitals: bfloat16 [24576, 2, 2048], P(('row', 'col')), may hold values from -6 to 6
- applied_orbitals: bfloat16 [24576, 2, 2048], P(('row', 'col')), may hold values from -6 to 6
- ritz_matrix: bfloat16 [2, 2048, 2048], P(None, 'row', 'col'), may hold values from -0.09375 to 0.09375
Outputs:
- rotated_orbitals: bfloat16 [24576, 2, 2048], P(('row', 'col'))
- rotated_applied: bfloat16 [24576, 2, 2048], P(('row', 'col'))
All inputs are finite; a program needn't handle non-finite values.
Results may differ from a plain program's by a relative error of at most 0.001.
Values may be sent and summed in bfloat16 or wider, within the bound.
A program may use at most 128 MiB of HBM per device.

v0:
```python
import jax
import jax.numpy as jnp
from jax import lax
from jax.sharding import PartitionSpec as P


def shards(orbitals, applied_orbitals, ritz_matrix):
    row_count = orbitals.shape[0]
    band_count = orbitals.shape[2]
    stacked = jnp.concatenate(
        [
            orbitals.reshape(row_count, 2 * band_count),
            applied_orbitals.reshape(row_count, 2 * band_count),
        ],
        0,
    )
    strip = lax.all_gather(ritz_matrix, "col", axis=2, tiled=True)
    shard_piece = lax.all_gather(strip, "row", axis=1, tiled=True)
    height = shard_piece.shape[1]
    real_cols = lax.slice_in_dim(stacked, 0, height, axis=1)
    imag_cols = lax.dynamic_slice_in_dim(stacked, band_count, height, 1)
    upper_half = jnp.concatenate([shard_piece[0], shard_piece[1]], 1)
    lower_half = jnp.concatenate([-shard_piece[1], shard_piece[0]], 1)
    running = jnp.dot(real_cols, upper_half, preferred_element_type=jnp.float32)
    running = running + jnp.dot(imag_cols, lower_half, preferred_element_type=jnp.float32)
    result = running.reshape(2 * row_count, 2, band_count)
    result = result.astype(jnp.bfloat16)
    return (result[:row_count], result[row_count:])


def solution(mesh):
    in_specs = (P(("row", "col"), None, None), P(("row", "col"), None, None), P(None, "row", "col"))
    out_specs = (P(("row", "col"), None, None), P(("row", "col"), None, None))
    return jax.shard_map(shards, mesh=mesh, in_specs=in_specs, out_specs=out_specs, check_vma=False)
```

profile of v0, /device:TPU:1, one launch (start us, length us, event | category | flops | bytes accessed | tf_op | source)
XLA Modules:
  0.0 229.9 jit_solution(4716080918865581641)
XLA Ops:
  7.2 0.0 all-gather.3.cloned.1.call-start
  7.2 0.7 all-gather.3.cloned.1.call-update
  7.9 0.0 all-gather.5.cloned.1.call-start
  7.9 43.9 %all-gather.3.cloned.1.call-done = bf16[2,128,2048]{2,1,0:T(8,128)(2,1)} async-done(((bf16[2,128,256]{2,1,0:T(8,128)(2,1)}), bf16[2,128,2048]{2,1,0:T(8,128)(2,1)}) %all-gather.3.cloned.1.call-update) | async-done | bytes 1048592 | tf_op jit(solution)/shard_map/all_gather | solution.py:17
  51.8 0.0 all-gather.5.cloned.1.call-update
  51.8 2.1 copy.5
  53.9 2.1 copy.6
  55.9 0.1 constant_dynamic-update-slice_fusion.1
  56.1 0.1 constant_dynamic-update-slice_fusion
  56.2 114.2 %all-gather.5.cloned.1.call-done = bf16[2,2048,2048]{2,1,0:T(8,128)(2,1)} async-done(((bf16[2,128,2048]{2,1,0:T(8,128)(2,1)}), bf16[2,2048,2048]{2,1,0:T(8,128)(2,1)}) %all-gather.5.cloned.1.call-update) | async-done | bytes 16777232 | tf_op jit(solution)/shard_map/all_gather | solution.py:18
  170.4 11.8 %slice_bitcast_fusion.1 = (bf16[2048,2048]{1,0:T(8,128)(2,1)}, bf16[2048,2048]{1,0:T(8,128)(2,1)}) fusion(bf16[2,2048,2048]{2,1,0:T(8,128)(2,1)} %all-gather.5.cloned.1.call-done), kind=kLoop, calls=%fused_computation.9 | loop fusion | bytes 33554432 | tf_op jit(solution)/shard_map/squeeze | solution.py:22
  182.2 12.6 %fusion = f32[384,4096]{1,0:T(8,128)} fusion(bf16[2048,2048]{1,0:T(8,128)(2,1)} %get-tuple-element.3, bf16[2048,2048]{1,0:T(8,128)(2,1)} %get-tuple-element.2, bf16[384,4096]{1,0:T(8,128)(2,1)S(1)} %constant_dynamic-update-slice_fusion), kind=kOutput, calls=%fused_computation | convolution fusion | flops 6476005376 | bytes 24641536 | tf_op jit(solution)/shard_map/dot_general | solution.py:24
  194.8 7.1 %fusion.14 = bf16[2048,2048]{1,0:T(8,128)(2,1)} fusion(bf16[2,2048,2048]{2,1,0:T(8,128)(2,1)} %all-gather.5.cloned.1.call-done), kind=kLoop, calls=%fused_computation.17 | loop fusion | flops 4194304 | bytes 16777216 | tf_op jit(solution)/shard_map/neg | solution.py:23
  201.9 14.3 %add_convert_fusion = bf16[384,4096]{1,0:T(8,128)(2,1)} fusion(f32[384,4096]{1,0:T(8,128)} %fusion, bf16[2048,2048]{1,0:T(8,128)(2,1)} %get-tuple-element.2, bf16[2048,2048]{1,0:T(8,128)(2,1)} %fusion.14, bf16[384,4096]{1,0:T(8,128)(2,1)S(1)} %constant_dynamic-update-slice_fusion), kind=kOutput, calls=%fused_computation.10 | convolution fusion | flops 6479151104 | bytes 27787264 | tf_op jit(solution)/shard_map/dot_general | solution.py:25
  216.2 2.1 fusion.15
  218.3 2.4 %slice.27 = bf16[192,2,2048]{2,1,0:T(2,128)(2,1)} reshape(bf16[192,4096]{1,0:T(8,128)(2,1)S(1)} %get-tuple-element.5) | data formatting | bytes 3145728 | tf_op jit(solution)/shard_map/slice | solution.py:28
  220.7 2.4 %slice.29 = bf16[192,2,2048]{2,1,0:T(2,128)(2,1)} reshape(bf16[192,4096]{1,0:T(8,128)(2,1)S(1)} %get-tuple-element.4) | data formatting | bytes 3145728 | tf_op jit(solution)/shard_map/slice | solution.py:28
Async XLA Ops:
  7.2 44.6 %all-gather.3.cloned.1.call-start = ((), (), s32[]{:S(2)}) async-start(), calls=%async_computation | async-start | bytes 1179648 | tf_op jit(solution)/shard_map/all_gather | solution.py:17
  7.9 162.5 %all-gather.5.cloned.1.call-start = ((), (), s32[]{:S(2)}) async-start(), calls=%async_computation.1 | async-start | bytes 17825792 | tf_op jit(solution)/shard_map/all_gather | solution.py:18
Sparse Core Ops, SparseCore 0:
  9.6 42.1 all-gather.2
  54.3 116.0 all-gather.4
where the time goes:
time: 230 us
  waiting for transfers between devices  159 us (69%)
  matrix products  26.9 us (12%)
  local copies, waits for them, and re-layouts  23 us (10%)
  between operations  14.1 us (6%)
  other arithmetic  7.14 us (3%)
    all_gather x1, waiting for transfers between devices, shards(): shard_piece = lax.all_gather(strip, 'row', axis=1, tiled=True)  114 us
    all_gather x1, waiting for transfers between devices, shards(): strip = lax.all_gather(ritz_matrix, 'col', axis=2, tiled=True)  43.9 us
    dot_general x1, matrix products, shards(): jnp.dot(imag_cols, lower_half, preferred_element_type=jnp.float32)  14.3 us
    dot_general x1, matrix products, shards(): running = jnp.dot(real_cols, upper_half, preferred_element_type=jnp.float32)  12.6 us
    squeeze x1, local copies, waits for them, and re-layouts, shards(): upper_half = jnp.concatenate([shard_piece[0], shard_piece[1]], 1)  11.8 us
    neg x1, other arithmetic, shards(): lower_half = jnp.concatenate([-shard_piece[1], shard_piece[0]], 1)  7.14 us
    slice x3, local copies, waits for them, and re-layouts, shards(): return (result[:row_count], result[row_count:])  6.8 us
  transfers between devices with their start and end apart: 2, of which 2 were waited for; matrix products, arithmetic and copies ran while one was open for 2% of the time, Pallas kernels for 0%

commit v1 on v0

--- a/solution.py
+++ b/solution.py
@@ -14,7 +14,8 @@
         ],
         0,
     )
-    strip = lax.all_gather(ritz_matrix, "col", axis=2, tiled=True)
+    sent = jnp.stack([ritz_matrix] * lax.axis_size("col"))
+    strip = jnp.concatenate(lax.all_to_all(sent, "col", 0, 0), axis=2)
     shard_piece = lax.all_gather(strip, "row", axis=1, tiled=True)
     height = shard_piece.shape[1]
     real_cols = lax.slice_in_dim(stacked, 0, height, axis=1)

time: 230 us -> 216 us (0.939)
  waiting for transfers between devices: 159 us -> 124 us
  blocking collectives: 0 us -> 20.3 us
    all_gather x1 -> x0, waiting for transfers between devices: 43.9 us -> none  [shards(): strip = lax.all_gather(ritz_matrix, 'col', axis=2, tiled=True)]
    all_to_all x0 -> x1, blocking collectives: none -> 20.3 us  [shards(): strip = jnp.concatenate(lax.all_to_all(sent, 'col', 0, 0), axis=2)]
    all_gather x1, waiting for transfers between devices: 114 us -> 124 us  [shards(): shard_piece = lax.all_gather(strip, 'row', axis=1, tiled=True)]
  transfers between devices with their start and end apart: 2 -> 1, of which waited for: 2 -> 1; matrix products, arithmetic and copies ran while one was open for 2% -> 1% of each run, Pallas kernels for 0% -> 0%
where the time goes in v1:
time: 216 us
  waiting for transfers between devices  124 us (57%)
  matrix products  27.1 us (13%)
  local copies, waits for them, and re-layouts  22.6 us (10%)
  blocking collectives  20.3 us (9%)
  between operations  14.1 us (7%)
  other arithmetic  7.15 us (3%)
    all_gather x1, waiting for transfers between devices, shards(): shard_piece = lax.all_gather(strip, 'row', axis=1, tiled=True)  124 us
    all_to_all x1, blocking collectives, shards(): strip = jnp.concatenate(lax.all_to_all(sent, 'col', 0, 0), axis=2)  20.3 us
    dot_general x1, matrix products, shards(): jnp.dot(imag_cols, lower_half, preferred_element_type=jnp.float32)  14.4 us
    dot_general x1, matrix products, shards(): running = jnp.dot(real_cols, upper_half, preferred_element_type=jnp.float32)  12.7 us
    squeeze x1, local copies, waits for them, and re-layouts, shards(): upper_half = jnp.concatenate([shard_piece[0], shard_piece[1]], 1)  11.8 us
    neg x1, other arithmetic, shards(): lower_half = jnp.concatenate([-shard_piece[1], shard_piece[0]], 1)  7.15 us
    slice x3, local copies, waits for them, and re-layouts, shards(): return (result[:row_count], result[row_count:])  6.8 us
  transfers between devices with their start and end apart: 1, of which 1 were waited for; matrix products, arithmetic and copies ran while one was open for 1% of the time, Pallas kernels for 0%

profile of v1, /device:TPU:1, one launch (start us, length us, event | category | flops | bytes accessed | tf_op | source)
XLA Modules:
  0.0 215.5 jit_solution(11595532196975396021)
XLA Ops:
  7.2 0.0 copy-start
  7.2 0.0 copy-start.1
  7.2 0.0 all-gather.2.cloned.1.call-start
  7.2 1.2 copy.6
  8.4 0.2 stack.2
  8.6 20.3 %all_to_all.5 = bf16[8,2,128,256]{2,3,1,0:T(8,128)(2,1)S(1)} all-to-all(bf16[8,2,128,256]{2,3,1,0:T(8,128)(2,1)S(1)} %stack.2), channel_id=1, replica_groups=mesh['row'=16,'col'=8] {'col'}, dimensions={0} | all-to-all | bytes 2097152 | tf_op jit(solution)/shard_map/all_to_all | solution.py:18
  28.9 1.0 copy.7
  30.0 0.0 all-gather.2.cloned.1.call-update
  30.0 0.0 copy-done
  30.0 0.6 copy.8
  30.7 0.0 copy-done.1
  30.7 0.6 copy.9
  31.3 0.1 constant_dynamic-update-slice_fusion.1
  31.5 0.1 constant_dynamic-update-slice_fusion
  31.6 124.2 %all-gather.2.cloned.1.call-done = bf16[2,2048,2048]{1,2,0:T(8,128)(2,1)} async-done(((bf16[2,128,2048]{1,2,0:T(8,128)(2,1)}), bf16[2,2048,2048]{1,2,0:T(8,128)(2,1)}) %all-gather.2.cloned.1.call-update) | async-done | bytes 16777232 | tf_op jit(solution)/shard_map/all_gather | solution.py:19
  155.8 11.8 %slice_bitcast_fusion.1 = (bf16[2048,2048]{0,1:T(8,128)(2,1)}, bf16[2048,2048]{0,1:T(8,128)(2,1)}) fusion(bf16[2,2048,2048]{1,2,0:T(8,128)(2,1)} %all-gather.2.cloned.1.call-done), kind=kLoop, calls=%fused_computation.9 | loop fusion | bytes 33554432 | tf_op jit(solution)/shard_map/squeeze | solution.py:23
  167.6 12.7 %fusion = f32[384,4096]{1,0:T(8,128)} fusion(bf16[2048,2048]{0,1:T(8,128)(2,1)} %get-tuple-element.3, bf16[2048,2048]{0,1:T(8,128)(2,1)} %get-tuple-element.2, bf16[384,4096]{1,0:T(8,128)(2,1)S(1)} %constant_dynamic-update-slice_fusion), kind=kOutput, calls=%fused_computation | convolution fusion | flops 6476005376 | bytes 24641536 | tf_op jit(solution)/shard_map/dot_general | solution.py:25
  180.3 7.1 %fusion.14 = bf16[2048,2048]{0,1:T(8,128)(2,1)} fusion(bf16[2,2048,2048]{1,2,0:T(8,128)(2,1)} %all-gather.2.cloned.1.call-done), kind=kLoop, calls=%fused_computation.17 | loop fusion | flops 4194304 | bytes 16777216 | tf_op jit(solution)/shard_map/neg | solution.py:24
  187.5 14.4 %add_convert_fusion = bf16[384,4096]{1,0:T(8,128)(2,1)} fusion(f32[384,4096]{1,0:T(8,128)} %fusion, bf16[2048,2048]{0,1:T(8,128)(2,1)} %get-tuple-element.2, bf16[2048,2048]{0,1:T(8,128)(2,1)} %fusion.14, bf16[384,4096]{1,0:T(8,128)(2,1)S(1)} %constant_dynamic-update-slice_fusion), kind=kOutput, calls=%fused_computation.10 | convolution fusion | flops 6479151104 | bytes 27787264 | tf_op jit(solution)/shard_map/dot_general | solution.py:26
  201.9 2.1 fusion.15
  204.0 2.4 %slice.27 = bf16[192,2,2048]{2,1,0:T(2,128)(2,1)} reshape(bf16[192,4096]{1,0:T(8,128)(2,1)S(1)} %get-tuple-element.5) | data formatting | bytes 3145728 | tf_op jit(solution)/shard_map/slice | solution.py:29
  206.4 2.4 %slice.29 = bf16[192,2,2048]{2,1,0:T(2,128)(2,1)} reshape(bf16[192,4096]{1,0:T(8,128)(2,1)S(1)} %get-tuple-element.4) | data formatting | bytes 3145728 | tf_op jit(solution)/shard_map/slice | solution.py:29
Async XLA Ops:
  7.2 22.8 %copy-start = (bf16[192,2,2048]{2,1,0:T(2,128)(2,1)S(1)}, bf16[192,2,2048]{2,1,0:T(2,128)(2,1)}, u32[]{:S(2)}) copy-start(bf16[192,2,2048]{2,1,0:T(2,128)(2,1)} %param.3) | copy-start | bytes 4718596
  7.2 23.5 %copy-start.1 = (bf16[192,2,2048]{2,1,0:T(2,128)(2,1)S(1)}, bf16[192,2,2048]{2,1,0:T(2,128)(2,1)}, u32[]{:S(2)}) copy-start(bf16[192,2,2048]{2,1,0:T(2,128)(2,1)} %param.4) | copy-start | bytes 4718596
  7.2 148.6 %all-gather.2.cloned.1.call-start = ((), (), s32[]{:S(2)}) async-start(), calls=%async_computation.1 | async-start | bytes 17825792 | tf_op jit(solution)/shard_map/all_gather | solution.py:19
Sparse Core Ops, SparseCore 0:
  30.1 125.6 all-gather.1
